TPU v7x, 32 devices: a whole 2x2x4 slice. The times are simulated.
32 devices in a mesh: dp: 8 (over z, x), mp: 4 (over y, core).
Axes of the slice: x: 2, y: 2, z: 4, core: 2. Of those that a mesh axis runs over, the one named last changes fastest.
Arguments:
- hidden_in: bfloat16 [8, 2048, 960], P('dp', 'mp'), may hold values from -6 to 6
- cotangent: bfloat16 [8, 2048, 960], P('dp', 'mp'), may hold values from -6 to 6
- segments: int32 [8, 2048], P('dp'), may hold values from 0 to 3, never falling along the last dimension, each value on 1 to 1024 neighbouring positions
- positions: int32 [8, 2048], P('dp', 'mp'), may hold values from 0 to 4095
- attn_in: bfloat16 [960, 1600], P('dp', 'mp'), may hold values from -0.1875 to 0.1875
- attn_out: bfloat16 [960, 960], P('mp', 'dp'), may hold values from -0.75 to 0.75
- w_gate: bfloat16 [960, 2560], P('dp', 'mp'), may hold values from -0.1875 to 0.1875
- w_up: bfloat16 [960, 2560], P('dp', 'mp'), may hold values from -0.1875 to 0.1875
- w_down: bfloat16 [2560, 960], P('mp', 'dp'), may hold values from -0.125 to 0.125
- norm1_gain: bfloat16 [960], P('dp'), may hold values from 0.099609375 to 1.8984375
- norm2_gain: bfloat16 [960], P('dp'), may hold values from 0.099609375 to 1.8984375
Outputs:
- hidden_out: bfloat16 [8, 2048, 960], P('dp', 'mp')
- grad_hidden: float32 [8, 2048, 960], P('dp', 'mp')
- grad_attn_in: float32 [960, 1600], P('dp', 'mp')
- grad_attn_out: float32 [960, 960], P('mp', 'dp')
- grad_gate: float32 [960, 2560], P('dp', 'mp')
- grad_up: float32 [960, 2560], P('dp', 'mp')
- grad_down: float32 [2560, 960], P('mp', 'dp')
- grad_gain1: float32 [960], P('dp')
- grad_gain2: float32 [960], P('dp')
Inputs may be any that keep to these rules, and one draw needn't show every extreme that they name: `segments`: segment numbers never fall along a sequence; every segment is a run of 1 to 1024 tokens.
All inputs are finite; a program needn't handle non-finite values.
Results may differ from a plain program's by a relative error of at most 0.015.
Values may be sent and summed in bfloat16 or wider, within the bound.
A program may use at most 192 MiB of HBM per device.

v0:
```python
import math
import jax
import jax.numpy as jnp
from jax import lax
from jax.sharding import PartitionSpec as P

HEADS = 15
KV_HEADS = 5
HEAD_DIM = 64
EPSILON = 1e-05
SCORE_SCALE = 0.125
MASK_FILL = -1e30


def rms_forward(values_in, gain):
    inverse = lax.rsqrt(jnp.mean(values_in * values_in, axis=-1, keepdims=True) + EPSILON)
    return (values_in * inverse * gain, inverse)


def rms_backward(values_in, inverse, gain, upstream):
    scaled = upstream * gain
    grad_in = inverse * (
        scaled
        - values_in * inverse * inverse * jnp.mean(scaled * values_in, axis=-1, keepdims=True)
    )
    return (grad_in, jnp.sum(upstream * values_in * inverse, axis=0))


def rotary_tables(position_ids):
    half_dim = HEAD_DIM // 2
    frequency = jnp.exp(
        jnp.arange(half_dim, dtype=jnp.float32) * (-2.0 * math.log(10000.0) / HEAD_DIM)
    )
    angles = position_ids.astype(jnp.float32)[:, None] * frequency[None, :]
    return (jnp.cos(angles)[:, None, :], jnp.sin(angles)[:, None, :])


def rotate(tensor, cosine, sine):
    half_dim = HEAD_DIM // 2
    first, second = (tensor[..., :half_dim], tensor[..., half_dim:])
    return jnp.concatenate(
        [first * cosine - second * sine, second * cosine + first * sine], axis=-1
    )


def rotate_back(tensor, cosine, sine):
    half_dim = HEAD_DIM // 2
    first, second = (tensor[..., :half_dim], tensor[..., half_dim:])
    return jnp.concatenate(
        [first * cosine + second * sine, second * cosine - first * sine], axis=-1
    )


def score_block(queries, keys, allowed):
    scores = (
        jnp.einsum("grd,sd->grs", queries, keys, preferred_element_type=jnp.float32) * SCORE_SCALE
    )
    return jnp.where(allowed[None], scores, MASK_FILL)


def attend(queries, keys, values, allowed):
    scores = score_block(queries, keys, allowed)
    peak = jnp.max(scores, axis=-1, keepdims=True)
    total = jnp.sum(jnp.exp(scores - peak), axis=-1, keepdims=True)
    log_total = peak + jnp.log(total)
    probs = jnp.exp(scores - log_total).astype(jnp.bfloat16)
    output = jnp.einsum("grs,sd->grd", probs, values, preferred_element_type=jnp.float32)
    return (output, log_total[..., 0])


def attend_back(queries, keys, values, allowed, log_total, output_b, grad_out_b):
    scores = score_block(queries, keys, allowed)
    probs = jnp.exp(scores - log_total[..., None])
    probs_b = probs.astype(jnp.bfloat16)
    grad_probs = jnp.einsum("grd,sd->grs", grad_out_b, values, preferred_element_type=jnp.float32)
    delta = jnp.sum(
        grad_out_b.astype(jnp.float32) * output_b.astype(jnp.float32), axis=-1, keepdims=True
    )
    grad_scores = (probs * (grad_probs - delta)).astype(jnp.bfloat16)
    grad_q = (
        jnp.einsum("grs,sd->grd", grad_scores, keys, preferred_element_type=jnp.float32)
        * SCORE_SCALE
    )
    grad_k = (
        jnp.einsum("grs,grd->sd", grad_scores, queries, preferred_element_type=jnp.float32)
        * SCORE_SCALE
    )
    grad_v = jnp.einsum("grs,grd->sd", probs_b, grad_out_b, preferred_element_type=jnp.float32)
    return (grad_q, grad_k, grad_v)


def per_device(
    hidden_in,
    cotangent,
    segments,
    positions,
    attn_in,
    attn_out,
    w_gate,
    w_up,
    w_down,
    norm1_gain,
    norm2_gain,
):
    tok_rows = hidden_in.shape[1]
    model_size = lax.axis_size("mp")
    seq_rows = tok_rows * model_size
    model_rank = lax.axis_index("mp")
    group_size = HEADS // KV_HEADS
    query_cols = HEADS * HEAD_DIM
    kv_cols = KV_HEADS * HEAD_DIM
    gathered = (
        lax.all_gather(attn_in, "dp", axis=0, tiled=True),
        lax.all_gather(attn_out, "dp", axis=1, tiled=True),
        lax.all_gather(w_gate, "dp", axis=0, tiled=True),
        lax.all_gather(w_up, "dp", axis=0, tiled=True),
        lax.all_gather(w_down, "dp", axis=1, tiled=True),
        lax.all_gather(norm1_gain, "dp", axis=0, tiled=True),
        lax.all_gather(norm2_gain, "dp", axis=0, tiled=True),
    )
    qkv_weight, out_weight = (
        lax.all_gather(gathered[0], "mp", axis=1, tiled=True),
        lax.all_gather(gathered[1], "mp", axis=0, tiled=True),
    )
    gate_weight, up_weight, down_weight = (gathered[2], gathered[3], gathered[4])
    gain_one = gathered[5].astype(jnp.float32)
    gain_two = gathered[6].astype(jnp.float32)
    resid_in = hidden_in[0].astype(jnp.float32)
    normed1, inv_one = rms_forward(resid_in, gain_one)
    normed1_b = normed1.astype(jnp.bfloat16)
    projected = jnp.dot(normed1_b, qkv_weight, preferred_element_type=jnp.float32)
    cosine, sine = rotary_tables(positions[0])
    queries = rotate(
        projected[:, :query_cols].reshape(tok_rows, HEADS, HEAD_DIM), cosine, sine
    ).astype(jnp.bfloat16)
    keys_own = (
        rotate(
            projected[:, query_cols : query_cols + kv_cols].reshape(tok_rows, KV_HEADS, HEAD_DIM),
            cosine,
            sine,
        )
        .astype(jnp.bfloat16)
        .reshape(tok_rows, kv_cols)
    )
    values_own = projected[:, query_cols + kv_cols :].astype(jnp.bfloat16)
    keys_all, values_all = (
        lax.all_gather(keys_own, "mp", axis=0, tiled=True),
        lax.all_gather(values_own, "mp", axis=0, tiled=True),
    )
    seq_seg = segments[0]
    query_seg = lax.dynamic_slice_in_dim(seq_seg, model_rank * tok_rows, tok_rows, 0)
    query_index = model_rank * tok_rows + jnp.arange(tok_rows, dtype=jnp.int32)
    key_index = jnp.arange(seq_rows, dtype=jnp.int32)
    allowed = (query_seg[:, None] == seq_seg[None, :]) & (
        key_index[None, :] <= query_index[:, None]
    )
    query_groups = queries.reshape(tok_rows, KV_HEADS, group_size, HEAD_DIM).transpose(1, 2, 0, 3)
    key_groups = keys_all.reshape(seq_rows, KV_HEADS, HEAD_DIM).transpose(1, 0, 2)
    value_groups = values_all.reshape(seq_rows, KV_HEADS, HEAD_DIM).transpose(1, 0, 2)
    outputs, log_totals = lax.map(
        lambda pack: attend(pack[0], pack[1], pack[2], allowed),
        (query_groups, key_groups, value_groups),
    )
    out_groups = outputs.astype(jnp.bfloat16)
    attn_b = out_groups.transpose(2, 0, 1, 3).reshape(tok_rows, query_cols)
    middle = resid_in + jnp.dot(attn_b, out_weight, preferred_element_type=jnp.float32)
    normed2, inv_two = rms_forward(middle, gain_two)
    normed2_b = normed2.astype(jnp.bfloat16)
    seq_normed = lax.all_gather(normed2_b, "mp", axis=0, tiled=True)
    gate = jnp.dot(seq_normed, gate_weight, preferred_element_type=jnp.float32)
    upper = jnp.dot(seq_normed, up_weight, preferred_element_type=jnp.float32)
    sigma = jax.nn.sigmoid(gate)
    silu_gate = gate * sigma
    hidden_b = (silu_gate * upper).astype(jnp.bfloat16)
    ffn_out = lax.psum_scatter(
        jnp.dot(hidden_b, down_weight, preferred_element_type=jnp.float32).astype(jnp.bfloat16),
        "mp",
        scatter_dimension=0,
        tiled=True,
    ).astype(jnp.float32)
    hidden_out = (middle + ffn_out).astype(jnp.bfloat16)
    regathered = (
        lax.all_gather(attn_in, "dp", axis=0, tiled=True),
        lax.all_gather(attn_out, "dp", axis=1, tiled=True),
        lax.all_gather(w_gate, "dp", axis=0, tiled=True),
        lax.all_gather(w_up, "dp", axis=0, tiled=True),
        lax.all_gather(w_down, "dp", axis=1, tiled=True),
        lax.all_gather(norm1_gain, "dp", axis=0, tiled=True),
        lax.all_gather(norm2_gain, "dp", axis=0, tiled=True),
    )
    qkv_weight, out_weight = (
        lax.all_gather(regathered[0], "mp", axis=1, tiled=True),
        lax.all_gather(regathered[1], "mp", axis=0, tiled=True),
    )
    gate_weight, up_weight, down_weight = (regathered[2], regathered[3], regathered[4])
    gain_one = regathered[5].astype(jnp.float32)
    gain_two = regathered[6].astype(jnp.float32)
    cot_local = cotangent[0]
    seq_cot = lax.all_gather(cot_local, "mp", axis=0, tiled=True)
    g_down = jnp.dot(hidden_b.T, seq_cot, preferred_element_type=jnp.float32)
    grad_hid = jnp.dot(seq_cot, down_weight.T, preferred_element_type=jnp.float32)
    grad_gate_act = (grad_hid * upper * sigma * (1.0 + gate * (1.0 - sigma))).astype(jnp.bfloat16)
    grad_up_act = (grad_hid * silu_gate).astype(jnp.bfloat16)
    g_gate = jnp.dot(seq_normed.T, grad_gate_act, preferred_element_type=jnp.float32)
    g_up = jnp.dot(seq_normed.T, grad_up_act, preferred_element_type=jnp.float32)
    grad_norm2 = lax.psum_scatter(
        jnp.dot(grad_gate_act, gate_weight.T, preferred_element_type=jnp.float32)
        + jnp.dot(grad_up_act, up_weight.T, preferred_element_type=jnp.float32),
        "mp",
        scatter_dimension=0,
        tiled=True,
    )
    grad_mid_norm, g_gain2 = rms_backward(middle, inv_two, gain_two, grad_norm2)
    grad_middle = cot_local.astype(jnp.float32) + grad_mid_norm
    middle_b = grad_middle.astype(jnp.bfloat16)
    g_out = jnp.dot(attn_b.T, middle_b, preferred_element_type=jnp.float32)
    grad_attn_b = jnp.dot(middle_b, out_weight.T, preferred_element_type=jnp.float32).astype(
        jnp.bfloat16
    )
    grad_groups = grad_attn_b.reshape(tok_rows, KV_HEADS, group_size, HEAD_DIM).transpose(
        1, 2, 0, 3
    )
    grad_q, grad_k, grad_v = lax.map(
        lambda pack: attend_back(pack[0], pack[1], pack[2], allowed, pack[3], pack[4], pack[5]),
        (query_groups, key_groups, value_groups, log_totals, out_groups, grad_groups),
    )
    key_grads, value_grads = (
        lax.psum_scatter(grad_k, "mp", scatter_dimension=1, tiled=True),
        lax.psum_scatter(grad_v, "mp", scatter_dimension=1, tiled=True),
    )
    grad_q = rotate_back(
        grad_q.transpose(2, 0, 1, 3).reshape(tok_rows, HEADS, HEAD_DIM), cosine, sine
    )
    key_grads = rotate_back(key_grads.transpose(1, 0, 2), cosine, sine)
    value_grads = value_grads.transpose(1, 0, 2)
    grad_proj = jnp.concatenate(
        [
            grad_q.reshape(tok_rows, query_cols),
            key_grads.reshape(tok_rows, kv_cols),
            value_grads.reshape(tok_rows, kv_cols),
        ],
        axis=1,
    ).astype(jnp.bfloat16)
    g_in = jnp.dot(normed1_b.T, grad_proj, preferred_element_type=jnp.float32)
    grad_norm1 = jnp.dot(grad_proj, qkv_weight.T, preferred_element_type=jnp.float32)
    grad_in_norm, g_gain1 = rms_backward(resid_in, inv_one, gain_one, grad_norm1)
    grad_input = grad_middle + grad_in_norm
    reduced = (
        lax.psum_scatter(g_in, "dp", scatter_dimension=0, tiled=True),
        lax.psum_scatter(g_out, "dp", scatter_dimension=1, tiled=True),
        lax.psum_scatter(g_gate, "dp", scatter_dimension=0, tiled=True),
        lax.psum_scatter(g_up, "dp", scatter_dimension=0, tiled=True),
        lax.psum_scatter(g_down, "dp", scatter_dimension=1, tiled=True),
        lax.psum_scatter(g_gain1, "dp", scatter_dimension=0, tiled=True),
        lax.psum_scatter(g_gain2, "dp", scatter_dimension=0, tiled=True),
    )
    grad_attn_in, grad_attn_out = (
        lax.psum_scatter(reduced[0], "mp", scatter_dimension=1, tiled=True),
        lax.psum_scatter(reduced[1], "mp", scatter_dimension=0, tiled=True),
    )
    grad_gain1, grad_gain2 = lax.psum((reduced[5], reduced[6]), "mp")
    return (
        hidden_out[None],
        grad_input[None],
        grad_attn_in,
        grad_attn_out,
        reduced[2],
        reduced[3],
        reduced[4],
        grad_gain1,
        grad_gain2,
    )


def solution(mesh):
    return jax.shard_map(
        per_device,
        mesh=mesh,
        in_specs=(
            P("dp", "mp", None),
            P("dp", "mp", None),
            P("dp", None),
            P("dp", "mp"),
            P("dp", "mp"),
            P("mp", "dp"),
            P("dp", "mp"),
            P("dp", "mp"),
            P("mp", "dp"),
            P("dp"),
            P("dp"),
        ),
        out_specs=(
            P("dp", "mp", None),
            P("dp", "mp", None),
            P("dp", "mp"),
            P("mp", "dp"),
            P("dp", "mp"),
            P("dp", "mp"),
            P("mp", "dp"),
            P("dp"),
            P("dp"),
        ),
        check_vma=False,
    )
```

profile of v0, /device:TPU:0, one launch (start us, length us, event | category | flops | bytes accessed | tf_op | source)
XLA Modules:
  0.0 1195.8 jit_solution(7193035129277229926)
XLA Ops:
  7.3 34.3 %all-gather.1 = bf16[8,120,400]{1,2,0:T(8,128)(2,1)S(1)} all-gather(bf16[1,120,400]{1,2,0:T(8,128)(2,1)} %bitcast.241), channel_id=1, replica_groups=mesh['dp'=8,'mp'=4] {'dp'}, dimensions={0}, use_global_device_ids=true | all-gather | bytes 864000 | tf_op jit(solution)/shard_map/all_gather | solution.py:113
  45.2 21.3 %all-reduce.10 = (bf16[960]{0:T(1024)(128)(2,1)S(1)}, bf16[960]{0:T(1024)(128)(2,1)S(1)}) all-reduce(bf16[960]{0:T(1024)(128)(2,1)S(1)} %dynamic-update-slice, bf16[960]{0:T(1024)(128)(2,1)S(1)} %dynamic-update-slice.1), channel_id=1, replica_groups=mesh['dp'=8,'mp'=4] {'dp'}, use_global_device_ids=true, to_apply=%add | all-reduce | flops 1920 | bytes 7680
  80.2 33.2 %all_gather.53 = bf16[240,960]{0,1:T(8,128)(2,1)} all-gather(bf16[240,120]{0,1:T(8,128)(2,1)S(1)} %copy.27), channel_id=1, replica_groups=mesh['dp'=8,'mp'=4] {'dp'}, dimensions={1}, use_global_device_ids=true | all-gather | bytes 518400 | tf_op jit(solution)/shard_map/all_gather | solution.py:114
  117.5 114.8 %while.30 = (s32[]{:T(128)}, bf16[5,3,512,64]{2,3,1,0:T(8,128)(2,1)S(1)}, f32[5,3,512]{2,1,0:T(4,128)S(1)}, bf16[5,3,512,64]{2,3,1,0:T(8,128)(2,1)S(1)}, bf16[5,...) while((s32[]{:T(128)}, ...), condition=%wide.region_4.5_spmd.clone.clone, body=%wide.region_1.4_spmd.clone.sunk.clone | while | flops 843053568 | bytes 43130984 | solution.py:160
  240.1 30.8 %all-gather.20.cloned.1.call-done = bf16[2048,960]{0,1:T(8,128)(2,1)} async-done(((bf16[512,960]{0,1:T(8,128)(2,1)}), bf16[2048,960]{0,1:T(8,128)(2,1)}) %all-gather.20.cloned.1.call-update) | async-done | bytes 3932176 | tf_op jit(solution)/shard_map/all_gather | solution.py:169
  270.9 8.3 fusion.89
  279.2 35.4 %all-gather.22.cloned.1.call-done = bf16[960,640]{1,0:T(8,128)(2,1)} async-done(((bf16[120,640]{1,0:T(8,128)(2,1)}), bf16[960,640]{1,0:T(8,128)(2,1)}) %all-gather.22.cloned.1.call-update) | async-done | bytes 1228816 | tf_op jit(solution)/shard_map/all_gather | solution.py:115
  314.6 8.3 fusion.88
  322.9 34.1 %all-gather.26.cloned.1.call-done = bf16[640,960]{0,1:T(8,128)(2,1)} async-done(((bf16[640,120]{0,1:T(8,128)(2,1)}), bf16[640,960]{0,1:T(8,128)(2,1)}) %all-gather.26.cloned.1.call-update) | async-done | bytes 1228816 | tf_op jit(solution)/shard_map/all_gather | solution.py:117
  357.0 33.4 %all-gather.28.cloned.1.call-done = bf16[1,2048,960]{1,2,0:T(8,128)(2,1)} async-done(((bf16[1,512,960]{1,2,0:T(8,128)(2,1)}), bf16[1,2048,960]{1,2,0:T(8,128)(2,1)}) %all-gather.28.cloned.1.call-update) | async-done | bytes 3932176 | tf_op jit(solution)/shard_map/all_gather | solution.py:199
  390.4 12.7 %multiply_convert_fusion.1 = (bf16[2048,640]{1,0:T(8,128)(2,1)S(1)}, bf16[2048,640]{1,0:T(8,128)(2,1)S(1)}, bf16[2048,640]{1,0:T(8,128)(2,1)}) fusion(f32[2048,640]{1,0:T(8,128)} %fusion.88, f32[2048,640]{1,0:T(8,128)} %fusion.89, bf16[640,960]{0,1:T(8,128)(2,1)} %all-gather.26.cloned.1.call-done, bf16[1,2048,960]{1,2,0:T(8,128)(2,1)} %all-gather.28.cloned.1.call-done), kind=kOutput, calls=%fused_computation.66 | convolution fusion | flops 2536243200 | bytes 23511040 | tf_op jit(solution)/shard_map/dot_general | solution.py:201
  419.3 61.8 %reduce-scatter.26.cloned.1.call-done = f32[512,960]{0,1:T(8,128)} async-done(((f32[2048,960]{0,1:T(8,128)}), f32[512,960]{0,1:T(8,128)}) %reduce-scatter.26.cloned.1.call-update) | async-done | bytes 1966096 | tf_op jit(solution)/shard_map/reduce_scatter | solution.py:206
  483.8 42.9 %reduce-scatter.24.cloned.1.call-done = bf16[512,960]{0,1:T(8,128)(2,1)} async-done(((bf16[2048,960]{0,1:T(8,128)(2,1)}), bf16[512,960]{0,1:T(8,128)(2,1)}) %reduce-scatter.24.cloned.1.call-update) | async-done | bytes 983056 | tf_op jit(solution)/shard_map/reduce_scatter | solution.py:175
  531.9 101.6 %while.31 = (s32[]{:T(128)}, f32[5,3,512,64]{2,3,1,0:T(8,128)}, f32[5,2048,64]{1,2,0:T(8,128)}, f32[5,2048,64]{1,2,0:T(8,128)}, bf16[5,3,512,64]{2,3,1,0:T(8,128...) while((s32[]{:T(128)}, f32[5,3,512,64]{2,3,1,0:T(8,128)}, ...), condition=%wide.region_11.12_spmd.clone.clone, body=%wide.region_9.11_spmd.clone.sunk.clone | while | flops 2048489984 | bytes 63237260 | solution.py:223
  641.9 26.4 %reduce-scatter.30.cloned.1.call-done = f32[5,512,64]{1,2,0:T(8,128)} async-done(((f32[5,2048,64]{1,2,0:T(8,128)}), f32[5,512,64]{1,2,0:T(8,128)}) %reduce-scatter.30.cloned.1.call-update) | async-done | bytes 655376 | tf_op jit(solution)/shard_map/reduce_scatter | solution.py:229
  670.2 35.5 %reduce-scatter.28.cloned.1.call-done = f32[5,512,64]{1,2,0:T(8,128)} async-done(((f32[5,2048,64]{1,2,0:T(8,128)}), f32[5,512,64]{1,2,0:T(8,128)}) %reduce-scatter.28.cloned.1.call-update) | async-done | bytes 655376 | tf_op jit(solution)/shard_map/reduce_scatter | solution.py:228
  736.1 57.5 %reduce-scatter.36.cloned.1.call-done = f32[120,960]{1,0:T(8,128)} async-done(((f32[960,960]{1,0:T(8,128)}), f32[120,960]{1,0:T(8,128)}) %reduce-scatter.36.cloned.1.call-update) | async-done | bytes 460816
  796.0 122.4 %reduce-scatter.38.cloned.1.call-done = f32[120,1600]{1,0:T(8,128)} async-done(((f32[960,1600]{1,0:T(8,128)}), f32[120,1600]{1,0:T(8,128)}) %reduce-scatter.38.cloned.1.call-update) | async-done | bytes 768016
  927.2 20.1 %all-reduce.8 = (f32[960]{0:T(1024)S(1)}, f32[960]{0:T(1024)S(1)}) all-reduce(f32[960]{0:T(1024)S(1)} %get-tuple-element.203, f32[960]{0:T(1024)S(1)} %copy-done.14), channel_id=14, replica_groups=mesh['dp'=8,'mp'=4] {'dp'}, use_global_device_ids=true, to_apply=%region_23.24.clone | all-reduce | flops 1920 | bytes 15360
  957.3 34.7 %reduce-scatter.44.cloned.1.call-done = f32[640,120]{0,1:T(8,128)} async-done(((f32[640,960]{0,1:T(8,128)}), f32[640,120]{0,1:T(8,128)}) %reduce-scatter.44.cloned.1.call-update) | async-done | bytes 307216
  992.0 73.3 %reduce-scatter.40.cloned.1.call-done = f32[120,640]{1,0:T(8,128)} async-done(((f32[960,640]{1,0:T(8,128)}), f32[120,640]{1,0:T(8,128)}) %reduce-scatter.40.cloned.1.call-update) | async-done | bytes 307216
  1065.3 73.2 %reduce-scatter.42.cloned.1.call-done = f32[120,640]{1,0:T(8,128)} async-done(((f32[960,640]{1,0:T(8,128)}), f32[120,640]{1,0:T(8,128)}) %reduce-scatter.42.cloned.1.call-update) | async-done | bytes 307216
  1138.5 23.6 %reduce-scatter.32.cloned.1.call-done = f32[240,120]{1,0:T(8,128)} async-done(((f32[960,120]{1,0:T(8,128)}), f32[240,120]{1,0:T(8,128)}) %reduce-scatter.32.cloned.1.call-update) | async-done | bytes 115216 | tf_op jit(solution)/shard_map/reduce_scatter | solution.py:259
  1162.1 26.6 %reduce-scatter.34.cloned.1.call-done = f32[400,120]{1,0:T(8,128)} async-done(((f32[1600,120]{1,0:T(8,128)}), f32[400,120]{1,0:T(8,128)}) %reduce-scatter.34.cloned.1.call-update) | async-done | bytes 192016
  (222 shorter events, 329.0 us)
Async XLA Ops:
  7.2 59.3 %copy-start.5 = (bf16[1,512,960]{1,2,0:T(8,128)(2,1)S(1)}, bf16[1,512,960]{1,2,0:T(8,128)(2,1)}, u32[]{:S(2)}) copy-start(bf16[1,512,960]{1,2,0:T(8,128)(2,1)} %param.15) | copy-start | bytes 2949124
  7.2 66.5 %all-gather.12.cloned.1.call-start = ((), (), s32[]{:S(2)}) async-start(), calls=%async_computation.11 | async-start | bytes 4096000 | tf_op jit(solution)/shard_map/all_gather | solution.py:122
  43.4 74.1 %all-gather.16.cloned.1.call-start = ((), (), s32[]{:S(2)}) async-start(), calls=%async_computation.13 | async-start | bytes 1638400 | tf_op jit(solution)/shard_map/all_gather | solution.py:148
  78.7 38.8 %all-gather.14.cloned.1.call-start = ((), (), s32[]{:S(2)}) async-start(), calls=%async_computation.12 | async-start | bytes 1638400 | tf_op jit(solution)/shard_map/all_gather | solution.py:147
  80.1 152.3 %all-gather.18.cloned.1.call-start = ((), (), s32[]{:S(2)}) async-start(), calls=%async_computation.14 | async-start | bytes 2457600 | tf_op jit(solution)/shard_map/all_gather | solution.py:123
  115.5 124.6 %all-gather.24.cloned.1.call-start = ((), (), s32[]{:S(2)}) async-start(), calls=%async_computation.17 | async-start | bytes 1382400 | tf_op jit(solution)/shard_map/all_gather | solution.py:116
  116.1 154.8 %all-gather.20.cloned.1.call-start = ((), (), s32[]{:S(2)}) async-start(), calls=%async_computation.15 | async-start | bytes 4915200 | tf_op jit(solution)/shard_map/all_gather | solution.py:169
  237.5 77.0 %all-gather.22.cloned.1.call-start = ((), (), s32[]{:S(2)}) async-start(), calls=%async_computation.16 | async-start | bytes 1382400 | tf_op jit(solution)/shard_map/all_gather | solution.py:115
  238.3 118.7 %all-gather.26.cloned.1.call-start = ((), (), s32[]{:S(2)}) async-start(), calls=%async_computation.18 | async-start | bytes 1382400 | tf_op jit(solution)/shard_map/all_gather | solution.py:117
  239.1 151.4 %all-gather.28.cloned.1.call-start = ((), (), s32[]{:S(2)}) async-start(), calls=%async_computation.24 | async-start | bytes 4915200 | tf_op jit(solution)/shard_map/all_gather | solution.py:199
  239.8 241.3 %reduce-scatter.26.cloned.1.call-start = ((), (), s32[]{:S(2)}) async-start(), calls=%async_computation.20 | async-start | bytes 9830400 | tf_op jit(solution)/shard_map/reduce_scatter | solution.py:206
  412.0 114.8 %reduce-scatter.24.cloned.1.call-start = ((), (), s32[]{:S(2)}) async-start(), calls=%async_computation.19 | async-start | bytes 4915200 | tf_op jit(solution)/shard_map/reduce_scatter | solution.py:175
  419.2 249.1 %reduce-scatter.30.cloned.1.call-start = ((), (), s32[]{:S(2)}) async-start(), calls=%async_computation.22 | async-start | bytes 3276800 | tf_op jit(solution)/shard_map/reduce_scatter | solution.py:229
  633.5 72.2 %reduce-scatter.28.cloned.1.call-start = ((), (), s32[]{:S(2)}) async-start(), calls=%async_computation.21 | async-start | bytes 3276800 | tf_op jit(solution)/shard_map/reduce_scatter | solution.py:228
  634.2 159.4 %reduce-scatter.36.cloned.1.call-start = ((), (), s32[]{:S(2)}) async-start(), calls=%async_computation.26 | async-start | bytes 4423680
  638.2 280.3 %reduce-scatter.38.cloned.1.call-start = ((), (), s32[]{:S(2)}) async-start(), calls=%async_computation.27 | async-start | bytes 7188480
  640.9 66.1 %copy-start.6 = (bf16[1,512,960]{1,2,0:T(8,128)(2,1)S(1)}, bf16[1,512,960]{1,2,0:T(8,128)(2,1)}, u32[]{:S(2)}) copy-start(bf16[1,512,960]{1,2,0:T(8,128)(2,1)} %param.15) | copy-start | bytes 2949124
  640.9 66.1 %copy-start.16 = (f32[960]{0:T(1024)S(1)}, f32[960]{0:T(1024)}, u32[]{:S(2)}) copy-start(f32[960]{0:T(1024)} %copy-done.15) | copy-start | bytes 11524
  640.9 66.1 %copy-start.18 = (f32[512]{0:T(512)S(1)}, f32[512]{0:T(512)}, u32[]{:S(2)}) copy-start(f32[512]{0:T(512)} %copy-done.17) | copy-start | bytes 6148
  713.0 279.0 %reduce-scatter.44.cloned.1.call-start = ((), (), s32[]{:S(2)}) async-start(), calls=%async_computation.30 | async-start | bytes 2764800
  720.6 344.7 %reduce-scatter.40.cloned.1.call-start = ((), (), s32[]{:S(2)}) async-start(), calls=%async_computation.28 | async-start | bytes 2764800
  728.3 410.2 %reduce-scatter.42.cloned.1.call-start = ((), (), s32[]{:S(2)}) async-start(), calls=%async_computation.29 | async-start | bytes 2764800
  736.0 426.0 %reduce-scatter.32.cloned.1.call-start = ((), (), s32[]{:S(2)}) async-start(), calls=%async_computation.23 | async-start | bytes 614400 | tf_op jit(solution)/shard_map/reduce_scatter | solution.py:259
  795.7 393.0 %reduce-scatter.34.cloned.1.call-start = ((), (), s32[]{:S(2)}) async-start(), calls=%async_computation.25 | async-start | bytes 1024000
  (23 other events, 337.1 us)
Sparse Core Ops, SparseCore 0:
  43.5 30.1 all-gather.11
  78.8 18.1 all-gather.15
  99.2 18.1 all-gather.13
  119.4 21.8 all-gather.17
  143.3 41.4 all-gather.23
  237.7 33.2 all-gather.19
  273.1 41.4 all-gather.21
  316.8 40.2 all-gather.25
  358.6 31.7 all-gather.27
  412.1 68.9 reduce-scatter.25
  483.8 42.8 reduce-scatter.23
  633.6 34.6 reduce-scatter.29
  671.0 34.6 reduce-scatter.27
  709.3 84.3 reduce-scatter.35
  797.5 120.8 reduce-scatter.37
  922.9 69.0 reduce-scatter.43
  996.5 68.8 reduce-scatter.39
  1069.8 68.6 reduce-scatter.41
  1141.7 20.2 reduce-scatter.31
  1165.2 23.4 reduce-scatter.33
where the time goes:
time: 1200 us
  waiting for transfers between devices  722 us (60%)
  matrix products  261 us (22%)
  blocking collectives  115 us (10%)
  other arithmetic  65.6 us (5%)
  between operations  16.4 us (1%)
  local copies, waits for them, and re-layouts  13.4 us (1%)
    unnamed x26, waiting for transfers between devices  391 us
    reduce_scatter x1, waiting for transfers between devices, per_device(): lax.psum_scatter(jnp.dot(grad_gate_act, gate_weight.T, preferred_element_...  61.8 us
    dot_general x10, matrix products, score_block(): jnp.einsum('grd,sd->grs', queries, keys, preferred_element_type=jnp.float32)  48.5 us
    reduce_scatter x1, waiting for transfers between devices, per_device(): lax.psum_scatter(jnp.dot(hidden_b, down_weight, preferred_element_type=jn...  42.9 us
    unnamed x2, blocking collectives  41.4 us
    dot_general x5, matrix products, attend(): jnp.einsum('grs,sd->grd', probs, values, preferred_element_type=jnp.float32)  40.2 us
    reduce_scatter x1, waiting for transfers between devices, per_device(): lax.psum_scatter(grad_k, 'mp', scatter_dimension=1, tiled=True)  35.5 us
    all_gather x1, waiting for transfers between devices, per_device(): lax.all_gather(w_gate, 'dp', axis=0, tiled=True)  35.4 us
  transfers between devices with their start and end apart: 20, of which 16 were waited for; matrix products, arithmetic and copies ran while one was open for 17% of the time, Pallas kernels for 0%

commit v1 on v0

--- a/solution.py
+++ b/solution.py
@@ -1,3 +1,4 @@
+import functools
 import math
 import jax
 import jax.numpy as jnp
@@ -10,6 +11,24 @@
 EPSILON = 1e-05
 SCORE_SCALE = 0.125
 MASK_FILL = -1e30
+
+
+def check_points(obj, axis_no):
+    stack_in = [obj]
+    n_all = lax.axis_size("dp")
+    for rr in range(1, n_all):
+        stack_in.append(
+            lax.ppermute(
+                stack_in[rr - 1],
+                axis_name="dp",
+                perm=[(src_i, (src_i - 1) % n_all) for src_i in range(n_all)],
+            )
+        )
+    v1 = jnp.concatenate(stack_in, axis=axis_no)
+    return jnp.roll(v1, lax.axis_index("dp") * obj.shape[axis_no], axis=axis_no)
+
+
+members_all_get = functools.partial(check_points, axis_no=0)
 
 
 def rms_forward(values_in, gain):
@@ -112,7 +131,7 @@
     gathered = (
         lax.all_gather(attn_in, "dp", axis=0, tiled=True),
         lax.all_gather(attn_out, "dp", axis=1, tiled=True),
-        lax.all_gather(w_gate, "dp", axis=0, tiled=True),
+        members_all_get(w_gate),
         lax.all_gather(w_up, "dp", axis=0, tiled=True),
         lax.all_gather(w_down, "dp", axis=1, tiled=True),
         lax.all_gather(norm1_gain, "dp", axis=0, tiled=True),

time: 1200 us -> 1140 us (0.950)
  waiting for transfers between devices: 722 us -> 612 us
  starting transfers between devices: 1.66 us -> 36.7 us
  local copies, waits for them, and re-layouts: 13.4 us -> 31.8 us
    ppermute x0 -> x7, starting transfers between devices: none -> 35.2 us  [check_points(): lax.ppermute(stack_in[rr - 1], axis_name='dp', perm=[(src_i, (src_i - 1)...]
    all_gather x1, waiting for transfers between devices: 34.1 us -> 0.01 us  [per_device(): lax.all_gather(w_down, 'dp', axis=1, tiled=True)]
    all_gather x1, waiting for transfers between devices: 33.4 us -> 0.01 us  [per_device(): seq_cot = lax.all_gather(cot_local, 'mp', axis=0, tiled=True)]
    all_gather x1, waiting for transfers between devices: 30.8 us -> 0.01 us  [per_device(): seq_normed = lax.all_gather(normed2_b, 'mp', axis=0, tiled=True)]
    all_gather x1, waiting for transfers between devices: 35.4 us -> 6.5 us  [per_device(): lax.all_gather(w_gate, 'dp', axis=0, tiled=True)]
    ppermute x0 -> x7, waiting for transfers between devices: none -> 20.3 us  [check_points(): lax.ppermute(stack_in[rr - 1], axis_name='dp', perm=[(src_i, (src_i - 1)...]
    unnamed x63 -> x90, local copies, waits for them, and re-layouts: 9.75 us -> 26.6 us
  transfers between devices with their start and end apart: 20 -> 27, of which waited for: 16 -> 18; matrix products, arithmetic and copies ran while one was open for 17% -> 20% of each run, Pallas kernels for 0% -> 0%
where the time goes in v1:
time: 1140 us
  waiting for transfers between devices  612 us (54%)
  matrix products  258 us (23%)
  blocking collectives  115 us (10%)
  other arithmetic  65.3 us (6%)
  starting transfers between devices  36.7 us (3%)
  local copies, waits for them, and re-layouts  31.8 us (3%)
  between operations  16.5 us (1%)
    unnamed x26, waiting for transfers between devices  390 us
    reduce_scatter x1, waiting for transfers between devices, per_device(): lax.psum_scatter(jnp.dot(grad_gate_act, gate_weight.T, preferred_element_...  60.6 us
    dot_general x10, matrix products, score_block(): jnp.einsum('grd,sd->grs', queries, keys, preferred_element_type=jnp.float32)  49 us
    reduce_scatter x1, waiting for transfers between devices, per_device(): lax.psum_scatter(jnp.dot(hidden_b, down_weight, preferred_element_type=jn...  42.9 us
    unnamed x2, blocking collectives  41.4 us
    dot_general x5, matrix products, attend(): jnp.einsum('grs,sd->grd', probs, values, preferred_element_type=jnp.float32)  40.5 us
    reduce_scatter x1, waiting for transfers between devices, per_device(): lax.psum_scatter(grad_k, 'mp', scatter_dimension=1, tiled=True)  35.6 us
    ppermute x7, starting transfers between devices, check_points(): lax.ppermute(stack_in[rr - 1], axis_name='dp', perm=[(src_i, (src_i - 1)...  35.2 us
  transfers between devices with their start and end apart: 27, of which 18 were waited for; matrix products, arithmetic and copies ran while one was open for 20% of the time, Pallas kernels for 0%

profile of v1, /device:TPU:0, one launch (start us, length us, event | category | flops | bytes accessed | tf_op | source)
XLA Modules:
  0.0 1136.7 jit_solution(12551509302215066943)
XLA Ops:
  7.3 34.3 %all-gather.1 = bf16[8,120,400]{1,2,0:T(8,128)(2,1)S(1)} all-gather(bf16[1,120,400]{1,2,0:T(8,128)(2,1)} %bitcast.238), channel_id=1, replica_groups=mesh['dp'=8,'mp'=4] {'dp'}, dimensions={0}, use_global_device_ids=true | all-gather | bytes 864000 | tf_op jit(solution)/shard_map/all_gather | solution.py:132
  45.2 21.3 %all-reduce.10 = (bf16[960]{0:T(1024)(128)(2,1)S(1)}, bf16[960]{0:T(1024)(128)(2,1)S(1)}) all-reduce(bf16[960]{0:T(1024)(128)(2,1)S(1)} %dynamic-update-slice, bf16[960]{0:T(1024)(128)(2,1)S(1)} %dynamic-update-slice.1), channel_id=1, replica_groups=mesh['dp'=8,'mp'=4] {'dp'}, use_global_device_ids=true, to_apply=%add | all-reduce | flops 1920 | bytes 7680
  80.2 33.2 %all_gather.52 = bf16[240,960]{0,1:T(8,128)(2,1)} all-gather(bf16[240,120]{0,1:T(8,128)(2,1)S(1)} %copy.27), channel_id=1, replica_groups=mesh['dp'=8,'mp'=4] {'dp'}, dimensions={1}, use_global_device_ids=true | all-gather | bytes 518400 | tf_op jit(solution)/shard_map/all_gather | solution.py:133
  119.6 115.1 %while.30 = (s32[]{:T(128)}, bf16[5,3,512,64]{2,3,1,0:T(8,128)(2,1)S(1)}, f32[5,3,512]{2,1,0:T(4,128)S(1)}, bf16[5,3,512,64]{2,3,1,0:T(8,128)(2,1)S(1)}, bf16[5,...) while((s32[]{:T(128)}, ...), condition=%wide.region_4.5_spmd.clone.clone, body=%wide.region_1.4_spmd.clone.sunk.clone | while | flops 843053568 | bytes 43130984 | solution.py:179
  134.6 8.1 fusion.161
  157.6 8.1 fusion.161
  180.5 8.0 fusion.161
  203.7 8.1 fusion.161
  226.6 8.2 fusion.161
  313.3 8.3 fusion.63
  327.7 9.4 multiply_convert_fusion.1
  361.8 60.6 %reduce-scatter.26.cloned.1.call-done = f32[512,960]{0,1:T(8,128)} async-done(((f32[2048,960]{0,1:T(8,128)}), f32[512,960]{0,1:T(8,128)}) %reduce-scatter.26.cloned.1.call-update) | async-done | bytes 1966096 | tf_op jit(solution)/shard_map/reduce_scatter | solution.py:225
  425.1 42.9 %reduce-scatter.24.cloned.1.call-done = bf16[512,960]{0,1:T(8,128)(2,1)} async-done(((bf16[2048,960]{0,1:T(8,128)(2,1)}), bf16[512,960]{0,1:T(8,128)(2,1)}) %reduce-scatter.24.cloned.1.call-update) | async-done | bytes 983056 | tf_op jit(solution)/shard_map/reduce_scatter | solution.py:194
  473.2 101.7 %while.31 = (s32[]{:T(128)}, f32[5,3,512,64]{2,3,1,0:T(8,128)}, f32[5,2048,64]{1,2,0:T(8,128)}, f32[5,2048,64]{1,2,0:T(8,128)}, bf16[5,3,512,64]{2,3,1,0:T(8,128...) while((s32[]{:T(128)}, f32[5,3,512,64]{2,3,1,0:T(8,128)}, ...), condition=%wide.region_11.12_spmd.clone.clone, body=%wide.region_9.11_spmd.clone.sunk.clone | while | flops 2048489984 | bytes 63237260 | solution.py:242
  583.4 26.4 %reduce-scatter.30.cloned.1.call-done = f32[5,512,64]{1,2,0:T(8,128)} async-done(((f32[5,2048,64]{1,2,0:T(8,128)}), f32[5,512,64]{1,2,0:T(8,128)}) %reduce-scatter.30.cloned.1.call-update) | async-done | bytes 655376 | tf_op jit(solution)/shard_map/reduce_scatter | solution.py:248
  611.6 35.6 %reduce-scatter.28.cloned.1.call-done = f32[5,512,64]{1,2,0:T(8,128)} async-done(((f32[5,2048,64]{1,2,0:T(8,128)}), f32[5,512,64]{1,2,0:T(8,128)}) %reduce-scatter.28.cloned.1.call-update) | async-done | bytes 655376 | tf_op jit(solution)/shard_map/reduce_scatter | solution.py:247
  677.7 57.4 %reduce-scatter.36.cloned.1.call-done = f32[120,960]{1,0:T(8,128)} async-done(((f32[960,960]{1,0:T(8,128)}), f32[120,960]{1,0:T(8,128)}) %reduce-scatter.36.cloned.1.call-update) | async-done | bytes 460816
  737.4 122.4 %reduce-scatter.38.cloned.1.call-done = f32[120,1600]{1,0:T(8,128)} async-done(((f32[960,1600]{1,0:T(8,128)}), f32[120,1600]{1,0:T(8,128)}) %reduce-scatter.38.cloned.1.call-update) | async-done | bytes 768016
  868.6 20.1 %all-reduce.8 = (f32[960]{0:T(1024)S(1)}, f32[960]{0:T(1024)S(1)}) all-reduce(f32[960]{0:T(1024)S(1)} %get-tuple-element.203, f32[960]{0:T(1024)S(1)} %copy-done.20), channel_id=14, replica_groups=mesh['dp'=8,'mp'=4] {'dp'}, use_global_device_ids=true, to_apply=%region_23.24.clone | all-reduce | flops 1920 | bytes 15360
  898.8 34.4 %reduce-scatter.44.cloned.1.call-done = f32[640,120]{0,1:T(8,128)} async-done(((f32[640,960]{0,1:T(8,128)}), f32[640,120]{0,1:T(8,128)}) %reduce-scatter.44.cloned.1.call-update) | async-done | bytes 307216
  933.2 73.1 %reduce-scatter.40.cloned.1.call-done = f32[120,640]{1,0:T(8,128)} async-done(((f32[960,640]{1,0:T(8,128)}), f32[120,640]{1,0:T(8,128)}) %reduce-scatter.40.cloned.1.call-update) | async-done | bytes 307216
  1006.3 73.1 %reduce-scatter.42.cloned.1.call-done = f32[120,640]{1,0:T(8,128)} async-done(((f32[960,640]{1,0:T(8,128)}), f32[120,640]{1,0:T(8,128)}) %reduce-scatter.42.cloned.1.call-update) | async-done | bytes 307216
  1079.4 23.6 %reduce-scatter.32.cloned.1.call-done = f32[240,120]{1,0:T(8,128)} async-done(((f32[960,120]{1,0:T(8,128)}), f32[240,120]{1,0:T(8,128)}) %reduce-scatter.32.cloned.1.call-update) | async-done | bytes 115216 | tf_op jit(solution)/shard_map/reduce_scatter | solution.py:278
  1103.0 26.6 %reduce-scatter.34.cloned.1.call-done = f32[400,120]{1,0:T(8,128)} async-done(((f32[1600,120]{1,0:T(8,128)}), f32[400,120]{1,0:T(8,128)}) %reduce-scatter.34.cloned.1.call-update) | async-done | bytes 192016
  (264 shorter events, 376.7 us)
Async XLA Ops:
  7.2 66.5 %all-gather.12.cloned.1.call-start = ((), (), s32[]{:S(2)}) async-start(), calls=%async_computation.11 | async-start | bytes 4096000 | tf_op jit(solution)/shard_map/all_gather | solution.py:141
  43.4 76.2 %all-gather.16.cloned.1.call-start = ((), (), s32[]{:S(2)}) async-start(), calls=%async_computation.13 | async-start | bytes 1638400 | tf_op jit(solution)/shard_map/all_gather | solution.py:167
  78.7 40.9 %all-gather.14.cloned.1.call-start = ((), (), s32[]{:S(2)}) async-start(), calls=%async_computation.12 | async-start | bytes 1638400 | tf_op jit(solution)/shard_map/all_gather | solution.py:166
  80.0 154.8 %all-gather.18.cloned.1.call-start = ((), (), s32[]{:S(2)}) async-start(), calls=%async_computation.14 | async-start | bytes 2457600 | tf_op jit(solution)/shard_map/all_gather | solution.py:142
  115.4 197.8 %all-gather.24.cloned.1.call-start = ((), (), s32[]{:S(2)}) async-start(), calls=%async_computation.17 | async-start | bytes 1382400 | tf_op jit(solution)/shard_map/all_gather | solution.py:136
  116.0 197.3 %all-gather.28.cloned.1.call-start = ((), (), s32[]{:S(2)}) async-start(), calls=%async_computation.24 | async-start | bytes 4915200 | tf_op jit(solution)/shard_map/all_gather | solution.py:218
  116.6 205.0 %all-gather.22.cloned.1.call-start = ((), (), s32[]{:S(2)}) async-start(), calls=%async_computation.16 | async-start | bytes 1382400 | tf_op jit(solution)/shard_map/all_gather | solution.py:135
  117.4 204.2 %all-gather.20.cloned.1.call-start = ((), (), s32[]{:S(2)}) async-start(), calls=%async_computation.15 | async-start | bytes 4915200 | tf_op jit(solution)/shard_map/all_gather | solution.py:188
  240.0 103.6 %all-gather.26.cloned.1.call-start = ((), (), s32[]{:S(2)}) async-start(), calls=%async_computation.19 | async-start | bytes 1382400 | tf_op jit(solution)/shard_map/all_gather | solution.py:204
  240.1 10.3 collective-permute-start
  251.0 11.2 collective-permute-start.1
  262.9 9.4 collective-permute-start.2
  272.3 9.0 collective-permute-start.3
  277.6 144.8 %reduce-scatter.26.cloned.1.call-start = ((), (), s32[]{:S(2)}) async-start(), calls=%async_computation.20 | async-start | bytes 9830400 | tf_op jit(solution)/shard_map/reduce_scatter | solution.py:225
  354.5 113.6 %reduce-scatter.24.cloned.1.call-start = ((), (), s32[]{:S(2)}) async-start(), calls=%async_computation.18 | async-start | bytes 4915200 | tf_op jit(solution)/shard_map/reduce_scatter | solution.py:194
  361.7 248.0 %reduce-scatter.30.cloned.1.call-start = ((), (), s32[]{:S(2)}) async-start(), calls=%async_computation.22 | async-start | bytes 3276800 | tf_op jit(solution)/shard_map/reduce_scatter | solution.py:248
  574.9 72.3 %reduce-scatter.28.cloned.1.call-start = ((), (), s32[]{:S(2)}) async-start(), calls=%async_computation.21 | async-start | bytes 3276800 | tf_op jit(solution)/shard_map/reduce_scatter | solution.py:247
  575.6 159.4 %reduce-scatter.36.cloned.1.call-start = ((), (), s32[]{:S(2)}) async-start(), calls=%async_computation.26 | async-start | bytes 4423680
  579.5 280.2 %reduce-scatter.38.cloned.1.call-start = ((), (), s32[]{:S(2)}) async-start(), calls=%async_computation.27 | async-start | bytes 7188480
  654.5 278.7 %reduce-scatter.44.cloned.1.call-start = ((), (), s32[]{:S(2)}) async-start(), calls=%async_computation.30 | async-start | bytes 2764800
  662.1 344.2 %reduce-scatter.40.cloned.1.call-start = ((), (), s32[]{:S(2)}) async-start(), calls=%async_computation.28 | async-start | bytes 2764800
  669.8 409.5 %reduce-scatter.42.cloned.1.call-start = ((), (), s32[]{:S(2)}) async-start(), calls=%async_computation.29 | async-start | bytes 2764800
  677.6 425.4 %reduce-scatter.32.cloned.1.call-start = ((), (), s32[]{:S(2)}) async-start(), calls=%async_computation.23 | async-start | bytes 614400 | tf_op jit(solution)/shard_map/reduce_scatter | solution.py:278
  737.1 392.5 %reduce-scatter.34.cloned.1.call-start = ((), (), s32[]{:S(2)}) async-start(), calls=%async_computation.25 | async-start | bytes 1024000
  (36 other events, 742.0 us)
Sparse Core Ops, SparseCore 0:
  43.5 30.1 all-gather.11
  78.8 18.1 all-gather.15
  99.2 18.1 all-gather.13
  119.4 21.8 all-gather.17
  143.3 41.4 all-gather.23
  186.2 31.8 all-gather.27
  220.2 45.8 all-gather.21
  268.3 31.6 all-gather.19
  302.1 41.4 all-gather.25
  354.6 67.7 reduce-scatter.25
  425.1 42.8 reduce-scatter.23
  575.0 34.6 reduce-scatter.29
  612.4 34.6 reduce-scatter.27
  650.7 84.2 reduce-scatter.35
  738.9 120.8 reduce-scatter.37
  864.3 68.9 reduce-scatter.43
  937.7 68.5 reduce-scatter.39
  1010.8 68.5 reduce-scatter.41
  1082.6 20.2 reduce-scatter.31
  1106.1 23.4 reduce-scatter.33
